TPU v7x, 256 devices: a whole 4x4x8 slice. The times are simulated.
256 devices in a mesh: col: 32 (over x, z_hi, core), row: 8 (over y, z_lo).
Axes of the slice: x: 4, y: 4, z: 8 (z_hi: 4, z_lo: 2; z = z_hi * 2 + z_lo), core: 2. Of those that a mesh axis runs over, the one named last changes fastest.
Arguments:
- weight: bfloat16 [8192, 53248], P('row', 'col'), may hold values from -6 to 6
- factor: float32 [1664, 53248], P('row', 'col'), may hold values from -1 to 2, as said below
- keep_mask: int32 [64, 13], P('row'), may hold values 0 or 1
Outputs:
- pruned: bfloat16 [8192, 53248], P('row', 'col')
Inputs may be any that keep to these rules, and one draw needn't show every extreme that they name: factor[i, k] = 0 for k < i; the diagonal entries factor[i, i] lie in [0.5, 2].
All inputs are finite; a program needn't handle non-finite values. No bound on the sum of `keep_mask` on one device may be relied on, other than what follows from the above.
Results may differ from a plain program's by a relative error of at most 0.0035.
Values may be sent and summed in bfloat16 or wider, within the bound.
No kernel may reach another device: no remote copies, remote signals or barrier semaphores. Data moves between devices by JAX's collectives and lax.ppermute only.
A program may use at most 192 MiB of HBM per device.

v0:
```python
from functools import partial
import jax
import jax.numpy as jnp
from jax import lax
from jax.sharding import PartitionSpec as P

PANW = 832
BLK = 128
PCOLS = 1664


def broadcast(x, axis, root):
    mine = lax.axis_index(axis) == root
    return lax.psum(jnp.where(mine, x, jnp.zeros_like(x)), axis)


def unit_inverse(strict, identity):
    width = strict.shape[0]
    result = identity - strict
    powered = strict
    reached = 2
    while reached < width:
        powered = jnp.dot(powered, powered, precision=lax.Precision.HIGHEST)
        result = jnp.dot(result, identity + powered, precision=lax.Precision.HIGHEST)
        reached = reached * 2
    return result


def prune_range(panel_state, keep_rows, diag_block, start_col, stop_col):
    sub_width = BLK // 2
    kept_parts = []
    error_parts = []
    identity = jnp.eye(sub_width, dtype=jnp.float32)
    for pan_start in range(start_col, stop_col, PANW):
        pan_stop = pan_start + PANW
        pieces = [
            panel_state[:, low : low + sub_width] for low in range(pan_start, pan_stop, sub_width)
        ]
        pan_errors = []
        for place in range(len(pieces)):
            sub_start = pan_start + place * sub_width
            sub_stop = sub_start + sub_width
            block_col = sub_start // BLK
            keep_col = jnp.repeat(
                keep_rows[:, block_col : block_col + 1].astype(jnp.float32), BLK, axis=0
            )
            dropped_col = 1.0 - keep_col
            columns = pieces[place]
            factor_sub = diag_block[sub_start:sub_stop, sub_start:sub_stop]
            pivots = jnp.diagonal(factor_sub)
            strict = jnp.triu(factor_sub, 1) / pivots[:, None]
            inverse = unit_inverse(strict, identity)
            solved = jnp.dot(columns, inverse, precision=lax.Precision.HIGHEST)
            current = jnp.where(dropped_col > 0.5, solved, columns)
            errors = dropped_col * current / pivots[None, :]
            kept_parts.append(keep_col * current)
            pan_errors.append(errors)
            if sub_stop < pan_stop:
                update = jnp.dot(
                    errors,
                    diag_block[sub_start:sub_stop, sub_stop:pan_stop],
                    precision=lax.Precision.HIGHEST,
                )
                for later in range(place + 1, len(pieces)):
                    offset = (later - place - 1) * sub_width
                    pieces[later] = pieces[later] - update[:, offset : offset + sub_width]
        pan_error = jnp.concatenate(pan_errors, axis=1)
        error_parts.append(pan_error)
        if pan_stop < PCOLS:
            later_update = jnp.dot(
                pan_error,
                diag_block[pan_start:pan_stop, pan_stop:],
                precision=lax.Precision.HIGHEST,
            )
            panel_state = jnp.concatenate(
                [panel_state[:, :pan_stop], panel_state[:, pan_stop:] - later_update], axis=1
            )
    return (panel_state, jnp.concatenate(kept_parts, axis=1), jnp.concatenate(error_parts, axis=1))


def skip_range(panel_state, keep_rows, diag_block, start_col, stop_col):
    blank = jnp.zeros((panel_state.shape[0], stop_col - start_col), jnp.float32)
    return (panel_state, blank, blank)


def per_device(weight, factor, keep_mask):
    section = lax.axis_index("col")
    owner = section == 0
    gathered = lax.all_gather(factor, "row", axis=0, tiled=True)
    factor_low = gathered.astype(jnp.bfloat16)
    panel_state = weight.astype(jnp.float32)
    panel_state, kept, error_all = lax.cond(
        owner,
        partial(prune_range, start_col=0, stop_col=PCOLS),
        partial(skip_range, start_col=0, stop_col=PCOLS),
        panel_state,
        keep_mask,
        gathered,
    )
    arrived = broadcast(error_all.astype(jnp.bfloat16), "col", 0)
    compensation = jnp.dot(arrived, factor_low, preferred_element_type=jnp.float32)
    section_width = weight.shape[1]
    global_cols = section * section_width + jnp.arange(section_width, dtype=jnp.int32)
    kept_padded = jnp.concatenate(
        [kept, jnp.zeros((kept.shape[0], section_width - PCOLS), jnp.float32)], axis=1
    )
    trailing = weight.astype(jnp.float32) - compensation
    return jnp.where((global_cols < PCOLS)[None, :], kept_padded, trailing).astype(jnp.bfloat16)


def solution(mesh):
    in_specs = (P("row", "col"), P("row", "col"), P("row", None))
    out_specs = P("row", "col")
    return jax.shard_map(
        per_device, mesh=mesh, in_specs=in_specs, out_specs=out_specs, check_vma=False
    )
```

profile of v0, /device:TPU:1, one launch (start us, length us, event | category | flops | bytes accessed | tf_op | source)
XLA Modules:
  0.0 870.4 jit_solution(3260335162966329133)
XLA Ops:
  6.5 0.0 all-gather.2.cloned.1.call-start
  6.5 0.7 all-gather.2.cloned.1.call-update
  7.3 0.0 all-reduce.2.cloned.1.call-start
  7.3 0.0 copy-start.64
  7.3 5.1 convert_element_type.409
  12.4 221.6 %all-gather.2.cloned.1.call-done = f32[1664,1664]{1,0:T(8,128)} async-done(((f32[208,1664]{1,0:T(8,128)}), f32[1664,1664]{1,0:T(8,128)}) %all-gather.2.cloned.1.call-update) | async-done | bytes 11075600 | tf_op jit(solution)/shard_map/all_gather | solution.py:89
  234.1 0.0 copy-done.64
  234.1 4.2 conditional.1
  234.1 2.2 broadcast.398
  236.3 2.0 broadcast.397.clone
  238.2 1.9 broadcast_select_fusion
  240.2 0.0 copy-start.6
  240.2 0.0 all-reduce.2.cloned.1.call-update
  240.2 609.3 %all-reduce.2.cloned.1.call-done = bf16[1024,1664]{0,1:T(8,128)(2,1)} async-done(((bf16[1024,1664]{0,1:T(8,128)(2,1)}), bf16[1024,1664]{0,1:T(8,128)(2,1)}) %all-reduce.2.cloned.1.call-update) | async-done | bytes 3407888 | tf_op jit(solution)/shard_map/psum | solution.py:14
  849.5 0.0 copy-done.6
  849.6 14.0 %select_convert_fusion = bf16[1024,1664]{1,0:T(8,128)(2,1)} fusion(bf16[1024,1664]{1,0:T(8,128)(2,1)} %get-tuple-element.27, pred[1664]{0:T(1024)(128)(4,1)S(1)} %add_compare_fusion, bf16[1024,1664]{0,1:T(8,128)(2,1)} %all-reduce.2.cloned.1.call-done, f32[1664,1664]{1,0:T(8,128)} %all-gather.2.cloned.1.call-done, bf16[1024,1664]{1,0:T(8,128)(2,1)S(1)} %copy-done.6), kind=kOutput, calls=%fused_computation.857 | convolution fusion | flops 5678579712 | bytes 24708736 | tf_op jit(solution)/shard_map/dot_general | solution.py:101
  (1 shorter events, 0.0 us)
Async XLA Ops:
  6.5 227.5 %all-gather.2.cloned.1.call-start = ((), (), s32[]{:S(2)}) async-start(), calls=%async_computation | async-start | bytes 12460032 | tf_op jit(solution)/shard_map/all_gather | solution.py:89
  7.3 842.3 %all-reduce.2.cloned.1.call-start = ((), (), s32[]{:S(2)}) async-start(), calls=%async_computation.1 | async-start | bytes 6815744 | tf_op jit(solution)/shard_map/psum | solution.py:14
  7.3 226.8 %copy-start.64 = (s32[8,13]{1,0:T(8,128)S(1)}, s32[8,13]{1,0:T(8,128)}, u32[]{:S(2)}) copy-start(s32[8,13]{1,0:T(8,128)} %param.7) | copy-start | bytes 1252
  240.2 609.4 %copy-start.6 = (bf16[1024,1664]{1,0:T(8,128)(2,1)S(1)}, bf16[1024,1664]{1,0:T(8,128)(2,1)}, u32[]{:S(2)}) copy-start(bf16[1024,1664]{1,0:T(8,128)(2,1)} %param.5) | copy-start | bytes 10223620
Sparse Core Ops, SparseCore 0:
  9.1 224.9 all-gather.1
  240.3 609.1 all-reduce.1
where the time goes:
time: 886 us; the launch traced here: 870 us
  waiting for transfers between devices  832 us (94%)
  matrix products  14 us (2%)
  between operations  13.4 us (2%)
    psum x1, waiting for transfers between devices, broadcast(): return lax.psum(jnp.where(mine, x, jnp.zeros_like(x)), axis)  609 us
    all_gather x1, waiting for transfers between devices, per_device(): gathered = lax.all_gather(factor, 'row', axis=0, tiled=True)  222 us
  transfers between devices with their start and end apart: 2, of which 2 were waited for; matrix products, arithmetic and copies ran while one was open for 1% of the time, Pallas kernels for 0%

commit v1 on v0

--- a/solution.py
+++ b/solution.py
@@ -3,6 +3,7 @@
 import jax.numpy as jnp
 from jax import lax
 from jax.sharding import PartitionSpec as P
+from jax.lax import all_to_all, axis_size
 
 PANW = 832
 BLK = 128
@@ -86,7 +87,10 @@
 def per_device(weight, factor, keep_mask):
     section = lax.axis_index("col")
     owner = section == 0
-    gathered = lax.all_gather(factor, "row", axis=0, tiled=True)
+    gathered = jnp.concatenate(
+        all_to_all(jnp.stack([factor for _ in range(axis_size("row"))], axis=0), "row", 0, 0),
+        axis=0,
+    )
     factor_low = gathered.astype(jnp.bfloat16)
     panel_state = weight.astype(jnp.float32)
     panel_state, kept, error_all = lax.cond(

time: 886 us -> 786 us (0.89)
  waiting for transfers between devices: 832 us -> 728 us
    all_gather x1 -> x0, waiting for transfers between devices: 222 us -> none  [per_device(): gathered = lax.all_gather(factor, 'row', axis=0, tiled=True)]
    all_to_all x0 -> x1, waiting for transfers between devices: none -> 118 us  [per_device(): all_to_all(jnp.stack([factor for _ in range(axis_size('row'))], axis=0),...]
  transfers between devices with their start and end apart: 2 -> 2, of which waited for: 2 -> 2; matrix products, arithmetic and copies ran while one was open for 1% -> 0% of each run, Pallas kernels for 0% -> 0%
where the time goes in v1:
time: 786 us; the launch traced here: 777 us
  waiting for transfers between devices  728 us (93%)
  matrix products  14 us (2%)
  between operations  13.4 us (2%)
  local copies, waits for them, and re-layouts  10.2 us (1%)
    psum x1, waiting for transfers between devices, broadcast(): return lax.psum(jnp.where(mine, x, jnp.zeros_like(x)), axis)  609 us
    all_to_all x1, waiting for transfers between devices, per_device(): all_to_all(jnp.stack([factor for _ in range(axis_size('row'))], axis=0),...  118 us
  transfers between devices with their start and end apart: 2, of which 2 were waited for; matrix products, arithmetic and copies ran while one was open for 0% of the time, Pallas kernels for 0%

profile of v1, /device:TPU:1, one launch (start us, length us, event | category | flops | bytes accessed | tf_op | source)
XLA Modules:
  0.0 777.2 jit_solution(2731687882761739966)
XLA Ops:
  6.5 6.1 stack.2
  12.6 0.0 copy-start.6
  12.6 6.6 all-to-all-start
  19.3 0.0 all-reduce.2.cloned.1.call-start
  19.3 0.0 copy-done.6
  19.3 0.0 copy-start.65
  19.3 3.3 convert_element_type.409
  22.6 118.3 %all-to-all-done = f32[8,208,1664]{2,1,0:T(8,128)} async-done(((f32[8,208,1664]{2,1,0:T(8,128)}), f32[8,208,1664]{2,1,0:T(8,128)}, u32[]{:S(2)}, u32[]{:S(2)}) %all-to-all-start) | async-done | bytes 11075616 | tf_op jit(solution)/shard_map/all_to_all | solution.py:91
  140.9 0.0 copy-done.65
  140.9 4.1 conditional.1
  140.9 2.1 broadcast.400
  143.0 2.0 broadcast.399.clone
  145.0 1.9 broadcast_select_fusion
  147.0 0.0 copy-start.7
  147.0 0.0 all-reduce.2.cloned.1.call-update
  147.0 609.3 %all-reduce.2.cloned.1.call-done = bf16[1024,1664]{0,1:T(8,128)(2,1)} async-done(((bf16[1024,1664]{0,1:T(8,128)(2,1)}), bf16[1024,1664]{0,1:T(8,128)(2,1)}) %all-reduce.2.cloned.1.call-update) | async-done | bytes 3407888 | tf_op jit(solution)/shard_map/psum | solution.py:15
  756.3 0.0 copy-done.7
  756.3 14.0 %select_convert_fusion = bf16[1024,1664]{1,0:T(8,128)(2,1)} fusion(bf16[1024,1664]{1,0:T(8,128)(2,1)} %get-tuple-element.27, pred[1664]{0:T(1024)(128)(4,1)S(1)} %add_compare_fusion, bf16[1024,1664]{0,1:T(8,128)(2,1)} %all-reduce.2.cloned.1.call-done, f32[1664,1664]{1,0:T(8,128)} %bitcast.28, bf16[1024,1664]{1,0:T(8,128)(2,1)S(1)} %copy-done.7), kind=kOutput, calls=%fused_computation.857 | convolution fusion | flops 5678579712 | bytes 24708736 | tf_op jit(solution)/shard_map/dot_general | solution.py:105
  (1 shorter events, 0.0 us)
Async XLA Ops:
  12.6 6.7 copy-start.6
  12.6 128.3 %all-to-all-start = ((f32[8,208,1664]{2,1,0:T(8,128)}), f32[8,208,1664]{2,1,0:T(8,128)}, u32[]{:S(2)}, u32[]{:S(2)}) async-start(f32[8,208,1664]{2,1,0:T(8,128)} %stack.2), calls=%async_computation | async-start | bytes 22151168 | tf_op jit(solution)/shard_map/all_to_all | solution.py:91
  19.3 737.0 %all-reduce.2.cloned.1.call-start = ((), (), s32[]{:S(2)}) async-start(), calls=%async_computation.1 | async-start | bytes 6815744 | tf_op jit(solution)/shard_map/psum | solution.py:15
  19.3 121.6 %copy-start.65 = (s32[8,13]{1,0:T(8,128)S(1)}, s32[8,13]{1,0:T(8,128)}, u32[]{:S(2)}) copy-start(s32[8,13]{1,0:T(8,128)} %param.7) | copy-start | bytes 1252
  147.0 609.3 %copy-start.7 = (bf16[1024,1664]{1,0:T(8,128)(2,1)S(1)}, bf16[1024,1664]{1,0:T(8,128)(2,1)}, u32[]{:S(2)}) copy-start(bf16[1024,1664]{1,0:T(8,128)(2,1)} %param.5) | copy-start | bytes 10223620
Sparse Core Ops, SparseCore 0:
  147.1 609.1 all-reduce.1
